TPU v7x, 32 devices: a whole 2x2x4 slice. The times are simulated.
32 devices in a mesh: dom: 16 (over z, y, x), tgt: 2 (over core).
Axes of the slice: x: 2, y: 2, z: 4, core: 2. Of those that a mesh axis runs over, the one named last changes fastest.
Arguments:
- positions: float32 [3, 16384], P(None, ('dom', 'tgt')), may hold values from -3 to 3
- normals: float32 [3, 16384], P(None, ('dom', 'tgt')), may hold values from -6 to 6
- weights: float32 [16384], P(('dom', 'tgt')), may hold values from 0.001 to 0.01
- density: float32 [32, 16384], P(None, ('dom', 'tgt')), may hold values from -6 to 6
- partners: int32 [16, 8], P('dom'), may hold values from 0 to 15, as said below
- band_list: int32 [16, 8, 8], P('dom'), may hold values from 0 to 7
- near_list: int32 [128, 24], P(('dom', 'tgt')), may hold values from 0 to 71
- near_count: int32 [128], P(('dom', 'tgt')), may hold values from 1 to 24, as said below
- singular: int32 [128, 24], P(('dom', 'tgt')), may hold values 0 or 1
Outputs:
- near_field: float32 [32, 16384], P(None, ('dom', 'tgt'))
Inputs may be any that keep to these rules, and one draw needn't show every extreme that they name: In each matching the partners pair the partitions (the partner of a partner is the partition itself, never itself), and the 8 partners of a partition are distinct. `near_count`: 24 is reached by some target tile in every draw.
All inputs are finite; a program needn't handle non-finite values. No bound on the sum of `singular` on one device may be relied on, other than what follows from the above.
Results may differ from a plain program's by a relative error of at most 0.0041.
Values sent between devices are 32-bit elements; how exact they have to be, the bound alone decides.
A program may use at most 64 MiB of HBM per device.

v0:
```python
import math
import jax
import jax.numpy as jnp
from jax import lax
from jax.sharding import PartitionSpec as P

TILE = 128
wave_number = 6.0
coupling = 1.5
narrow_core = 0.1
wide_core = 0.4


def build_kernel(target_pos, source, valid_mask, flag_row):
    offset = source[:, 0:3, :, None] - target_pos[:, :, None, :]
    core_width = jnp.where(flag_row > 0, wide_core, narrow_core)[:, None, None]
    distance = jnp.sqrt(jnp.sum(offset * offset, axis=1) + core_width * core_width)
    inverse = 1.0 / distance
    normal_part = jnp.sum(offset * source[:, 3:6, :, None], axis=1) * inverse
    radial = inverse / (4.0 * math.pi)
    cos_part = jnp.cos(wave_number * distance) * radial
    sin_part = jnp.sin(wave_number * distance) * radial
    weight_mask = source[:, 6, :, None] * valid_mask[:, None, None]
    kernel_re = weight_mask * (
        normal_part * (-cos_part * inverse - wave_number * sin_part) - coupling * sin_part
    )
    kernel_im = weight_mask * (
        normal_part * (wave_number * cos_part - sin_part * inverse) + coupling * cos_part
    )
    return jnp.concatenate([kernel_re, kernel_im], axis=1).astype(jnp.bfloat16)


def density_side(source):
    density_bf = source[:, 7:, :].astype(jnp.bfloat16)
    half_rows = density_bf.shape[1] // 2
    real_part = density_bf[:, :half_rows]
    imag_part = density_bf[:, half_rows:]
    upper = jnp.concatenate([real_part, -imag_part], axis=2)
    lower = jnp.concatenate([imag_part, real_part], axis=2)
    return jnp.concatenate([upper, lower], axis=1)


def shards(
    positions, normals, weights, density, partners, band_list, near_list, near_count, singular
):
    payload = jnp.concatenate([positions, normals, weights[None, :], density], axis=0)
    channels = payload.shape[0]
    local_tiles = payload.shape[1] // TILE
    whole_part = lax.all_gather(payload, "tgt", axis=1, tiled=True)
    part_tiles = whole_part.reshape(channels, -1, TILE).transpose(1, 0, 2)
    n_dom = lax.axis_size("dom")
    band_size = band_list.shape[2]
    my_partners = partners[0]
    send_slots = jnp.zeros((n_dom, band_size, channels, TILE), jnp.float32)
    send_slots = send_slots.at[my_partners].set(part_tiles[band_list[0]])
    arrived = lax.all_to_all(send_slots, "dom", split_axis=0, concat_axis=0, tiled=True)
    band_tiles = arrived[my_partners]
    source_pool = jnp.concatenate([part_tiles, band_tiles.reshape(-1, channels, TILE)], axis=0)
    target_pos = positions.reshape(3, local_tiles, TILE).transpose(1, 0, 2)
    pair_targets = jnp.concatenate([target_pos, target_pos], axis=0)

    def add_pair(pair_idx, totals):
        columns = lax.dynamic_slice_in_dim(near_list, 2 * pair_idx, 2, 1)
        flag_pair = lax.dynamic_slice_in_dim(singular, 2 * pair_idx, 2, 1)
        pick_idx = columns.T.reshape(-1)
        source = source_pool[pick_idx]
        entry_ids = 2 * pair_idx + jnp.arange(2, dtype=jnp.int32)
        valid_mask = (entry_ids[:, None] < near_count[None, :]).reshape(-1).astype(jnp.float32)
        kernel = build_kernel(pair_targets, source, valid_mask, flag_pair.T.reshape(-1))
        left_side = density_side(source)
        term_pairs = jnp.einsum(
            "brs,bst->brt", left_side, kernel, preferred_element_type=jnp.float32
        )
        return totals + term_pairs[:local_tiles] + term_pairs[local_tiles:]

    trip_count = (jnp.max(near_count) + 1) // 2
    start_sum = jnp.zeros((local_tiles, channels - 7, TILE), jnp.float32)
    totals = lax.fori_loop(0, trip_count, add_pair, start_sum)
    return totals.transpose(1, 0, 2).reshape(channels - 7, local_tiles * TILE)


def solution(mesh):
    in_specs = (
        P(None, ("dom", "tgt")),
        P(None, ("dom", "tgt")),
        P(("dom", "tgt")),
        P(None, ("dom", "tgt")),
        P("dom", None),
        P("dom", None, None),
        P(("dom", "tgt"), None),
        P(("dom", "tgt")),
        P(("dom", "tgt"), None),
    )
    out_specs = P(None, ("dom", "tgt"))
    return jax.shard_map(shards, mesh=mesh, in_specs=in_specs, out_specs=out_specs, check_vma=False)
```

profile of v0, /device:TPU:16, one launch (start us, length us, event | category | flops | bytes accessed | tf_op | source)
XLA Modules:
  0.0 140.2 jit_solution(14776132372673987182)
XLA Ops:
  0.0 0.9 pad_maximum_fusion.1
  0.9 1.9 %all_gather.3 = f32[39,1024]{1,0:T(8,128)S(1)} all-gather(f32[39,512]{1,0:T(8,128)S(1)} %pad_maximum_fusion.1), channel_id=1, replica_groups=mesh['dom'=16,'tgt'=2] {'tgt'}, dimensions={1}, use_global_device_ids=true | all-gather | bytes 239616 | tf_op jit(solution)/shard_map/all_gather | solution.py:49
  3.0 0.7 gather_fusion.1
  3.7 0.2 copy.29
  3.9 0.4 copy-done.5
  4.4 1.6 %broadcast_in_dim.16 = f32[16,8,39,128]{3,1,2,0:T(8,128)} broadcast(f32[]{:T(128)} %constant.16.clone.1), dimensions={} | broadcast | bytes 2555908 | tf_op jit(solution)/shard_map/broadcast_in_dim | solution.py:54
  6.0 3.1 %scatter_fusion = f32[16,8,39,128]{3,1,2,0:T(8,128)} fusion(f32[16,8,39,128]{3,1,2,0:T(8,128)} %broadcast_in_dim.16, s32[8]{0:T(128)S(1)} %fusion.19, f32[8,8,39,128]{3,1,2,0:T(8,128)S(1)} %copy.29), kind=kCustom, calls=%fused_computation.3 | custom fusion | bytes 3833888 | tf_op jit(solution)/shard_map/scatter | solution.py:55
  9.1 7.3 %all-to-all-start = ((f32[16,8,39,128]{3,1,2,0:T(8,128)}), f32[16,8,39,128]{3,1,2,0:T(8,128)S(1)}, u32[]{:S(2)}, u32[]{:S(2)}) async-start(f32[16,8,39,128]{3,1,2,0:T(8,128)} %scatter_fusion), calls=%async_computation | async-start | bytes 5111808 | tf_op jit(solution)/shard_map/all_to_all | solution.py:56
  16.4 0.6 reduce_max.9
  17.9 56.5 %all-to-all-done = f32[16,8,39,128]{3,1,2,0:T(8,128)S(1)} async-done(((f32[16,8,39,128]{3,1,2,0:T(8,128)}), f32[16,8,39,128]{3,1,2,0:T(8,128)S(1)}, u32[]{:S(2)}, u32[]{:S(2)}) %all-to-all-start) | async-done | bytes 2555936 | tf_op jit(solution)/shard_map/all_to_all | solution.py:56
  74.4 1.7 %gather_fusion.2 = f32[8,8,39,128]{3,1,2,0:T(8,128)} fusion(f32[16,8,39,128]{3,1,2,0:T(8,128)S(1)} %all-to-all-done, s32[1024]{0:T(1024)S(1)} %pad_clamp_fusion.1), kind=kCustom, calls=%fused_computation.2 | custom fusion | bytes 2555936 | tf_op jit(solution)/shard_map/gather | solution.py:57
  76.0 1.5 %copy.42 = f32[8,8,39,128]{3,1,0,2:T(8,128)S(1)} copy(f32[8,8,39,128]{3,1,2,0:T(8,128)} %gather_fusion.2) | data formatting | bytes 2555904 | tf_op jit(solution)/shard_map/gather | solution.py:57
  77.5 0.1 pad_maximum_fusion
  77.6 0.3 copy.33
  77.9 61.7 %while.10 = (s32[]{:T(128)}, f32[4,32,128]{2,1,0:T(8,128)S(1)}, s32[]{:T(128)}, s32[4,24]{0,1:T(8,128)S(1)}, f32[72,39,128]{2,1,0:T(8,128)S(1)}, /*index=5*/s32[...) while((s32[]{:T(128)}, f32[4,32,128]{2,1,0:T(8,128)S(1)}, ...), condition=%wide.region_5.6_spmd, body=%wide.region_2.5_spmd.sunk | while | flops 23290952 | bytes 4471535 | solution.py:78
  78.1 0.6 gather_fusion
  78.6 1.0 fusion.33
  80.0 2.7 %multiply_convert_fusion.3 = (bf16[8,128,128]{2,1,0:T(8,128)(2,1)S(1)}, bf16[8,128,128]{2,1,0:T(8,128)(2,1)S(1)}) fusion(f32[8,128,128]{2,1,0:T(8,128)S(1)} %get-tuple-element.169, f32[8,128,128]{2,1,0:T(8,128)S(1)} %get-tuple-element.170, f32[8]{0:T(128)S(1)} %mul.168, f32[8,128]{1,0:T(8,128)S(1)} %broadcast_multiply_fusion.2), kind=kLoop, calls=%fused_computation.13.clone.1 | loop fusion | flops 3145728 | bytes 1576992 | tf_op jit(solution)/shard_map/convert.1
  82.8 0.2 fusion.35
  83.2 0.6 gather_fusion
  83.8 1.0 fusion.33
  85.2 2.7 %multiply_convert_fusion.3 = (bf16[8,128,128]{2,1,0:T(8,128)(2,1)S(1)}, bf16[8,128,128]{2,1,0:T(8,128)(2,1)S(1)}) fusion(f32[8,128,128]{2,1,0:T(8,128)S(1)} %get-tuple-element.169, f32[8,128,128]{2,1,0:T(8,128)S(1)} %get-tuple-element.170, f32[8]{0:T(128)S(1)} %mul.168, f32[8,128]{1,0:T(8,128)S(1)} %broadcast_multiply_fusion.2), kind=kLoop, calls=%fused_computation.13.clone.1 | loop fusion | flops 3145728 | bytes 1576992 | tf_op jit(solution)/shard_map/convert.1
  88.0 0.2 fusion.35
  88.3 0.6 gather_fusion
  88.9 1.0 fusion.33
  90.3 2.7 %multiply_convert_fusion.3 = (bf16[8,128,128]{2,1,0:T(8,128)(2,1)S(1)}, bf16[8,128,128]{2,1,0:T(8,128)(2,1)S(1)}) fusion(f32[8,128,128]{2,1,0:T(8,128)S(1)} %get-tuple-element.169, f32[8,128,128]{2,1,0:T(8,128)S(1)} %get-tuple-element.170, f32[8]{0:T(128)S(1)} %mul.168, f32[8,128]{1,0:T(8,128)S(1)} %broadcast_multiply_fusion.2), kind=kLoop, calls=%fused_computation.13.clone.1 | loop fusion | flops 3145728 | bytes 1576992 | tf_op jit(solution)/shard_map/convert.1
  93.1 0.2 fusion.35
  93.5 0.6 gather_fusion
  94.1 1.0 fusion.33
  95.5 2.7 %multiply_convert_fusion.3 = (bf16[8,128,128]{2,1,0:T(8,128)(2,1)S(1)}, bf16[8,128,128]{2,1,0:T(8,128)(2,1)S(1)}) fusion(f32[8,128,128]{2,1,0:T(8,128)S(1)} %get-tuple-element.169, f32[8,128,128]{2,1,0:T(8,128)S(1)} %get-tuple-element.170, f32[8]{0:T(128)S(1)} %mul.168, f32[8,128]{1,0:T(8,128)S(1)} %broadcast_multiply_fusion.2), kind=kLoop, calls=%fused_computation.13.clone.1 | loop fusion | flops 3145728 | bytes 1576992 | tf_op jit(solution)/shard_map/convert.1
  98.2 0.2 fusion.35
  98.6 0.6 gather_fusion
  99.2 1.0 fusion.33
  100.6 2.7 %multiply_convert_fusion.3 = (bf16[8,128,128]{2,1,0:T(8,128)(2,1)S(1)}, bf16[8,128,128]{2,1,0:T(8,128)(2,1)S(1)}) fusion(f32[8,128,128]{2,1,0:T(8,128)S(1)} %get-tuple-element.169, f32[8,128,128]{2,1,0:T(8,128)S(1)} %get-tuple-element.170, f32[8]{0:T(128)S(1)} %mul.168, f32[8,128]{1,0:T(8,128)S(1)} %broadcast_multiply_fusion.2), kind=kLoop, calls=%fused_computation.13.clone.1 | loop fusion | flops 3145728 | bytes 1576992 | tf_op jit(solution)/shard_map/convert.1
  103.4 0.2 fusion.35
  103.8 0.6 gather_fusion
  104.3 1.0 fusion.33
  105.7 2.7 %multiply_convert_fusion.3 = (bf16[8,128,128]{2,1,0:T(8,128)(2,1)S(1)}, bf16[8,128,128]{2,1,0:T(8,128)(2,1)S(1)}) fusion(f32[8,128,128]{2,1,0:T(8,128)S(1)} %get-tuple-element.169, f32[8,128,128]{2,1,0:T(8,128)S(1)} %get-tuple-element.170, f32[8]{0:T(128)S(1)} %mul.168, f32[8,128]{1,0:T(8,128)S(1)} %broadcast_multiply_fusion.2), kind=kLoop, calls=%fused_computation.13.clone.1 | loop fusion | flops 3145728 | bytes 1576992 | tf_op jit(solution)/shard_map/convert.1
  108.5 0.2 fusion.35
  108.9 0.6 gather_fusion
  109.5 1.0 fusion.33
  110.9 2.7 %multiply_convert_fusion.3 = (bf16[8,128,128]{2,1,0:T(8,128)(2,1)S(1)}, bf16[8,128,128]{2,1,0:T(8,128)(2,1)S(1)}) fusion(f32[8,128,128]{2,1,0:T(8,128)S(1)} %get-tuple-element.169, f32[8,128,128]{2,1,0:T(8,128)S(1)} %get-tuple-element.170, f32[8]{0:T(128)S(1)} %mul.168, f32[8,128]{1,0:T(8,128)S(1)} %broadcast_multiply_fusion.2), kind=kLoop, calls=%fused_computation.13.clone.1 | loop fusion | flops 3145728 | bytes 1576992 | tf_op jit(solution)/shard_map/convert.1
  113.6 0.2 fusion.35
  114.0 0.6 gather_fusion
  114.6 1.0 fusion.33
  116.0 2.7 %multiply_convert_fusion.3 = (bf16[8,128,128]{2,1,0:T(8,128)(2,1)S(1)}, bf16[8,128,128]{2,1,0:T(8,128)(2,1)S(1)}) fusion(f32[8,128,128]{2,1,0:T(8,128)S(1)} %get-tuple-element.169, f32[8,128,128]{2,1,0:T(8,128)S(1)} %get-tuple-element.170, f32[8]{0:T(128)S(1)} %mul.168, f32[8,128]{1,0:T(8,128)S(1)} %broadcast_multiply_fusion.2), kind=kLoop, calls=%fused_computation.13.clone.1 | loop fusion | flops 3145728 | bytes 1576992 | tf_op jit(solution)/shard_map/convert.1
  118.8 0.2 fusion.35
  119.2 0.6 gather_fusion
  119.7 1.0 fusion.33
  121.1 2.7 %multiply_convert_fusion.3 = (bf16[8,128,128]{2,1,0:T(8,128)(2,1)S(1)}, bf16[8,128,128]{2,1,0:T(8,128)(2,1)S(1)}) fusion(f32[8,128,128]{2,1,0:T(8,128)S(1)} %get-tuple-element.169, f32[8,128,128]{2,1,0:T(8,128)S(1)} %get-tuple-element.170, f32[8]{0:T(128)S(1)} %mul.168, f32[8,128]{1,0:T(8,128)S(1)} %broadcast_multiply_fusion.2), kind=kLoop, calls=%fused_computation.13.clone.1 | loop fusion | flops 3145728 | bytes 1576992 | tf_op jit(solution)/shard_map/convert.1
  123.9 0.2 fusion.35
  124.3 0.6 gather_fusion
  124.9 1.0 fusion.33
  126.3 2.7 %multiply_convert_fusion.3 = (bf16[8,128,128]{2,1,0:T(8,128)(2,1)S(1)}, bf16[8,128,128]{2,1,0:T(8,128)(2,1)S(1)}) fusion(f32[8,128,128]{2,1,0:T(8,128)S(1)} %get-tuple-element.169, f32[8,128,128]{2,1,0:T(8,128)S(1)} %get-tuple-element.170, f32[8]{0:T(128)S(1)} %mul.168, f32[8,128]{1,0:T(8,128)S(1)} %broadcast_multiply_fusion.2), kind=kLoop, calls=%fused_computation.13.clone.1 | loop fusion | flops 3145728 | bytes 1576992 | tf_op jit(solution)/shard_map/convert.1
  129.1 0.2 fusion.35
  129.4 0.6 gather_fusion
  130.0 1.0 fusion.33
  131.4 2.7 %multiply_convert_fusion.3 = (bf16[8,128,128]{2,1,0:T(8,128)(2,1)S(1)}, bf16[8,128,128]{2,1,0:T(8,128)(2,1)S(1)}) fusion(f32[8,128,128]{2,1,0:T(8,128)S(1)} %get-tuple-element.169, f32[8,128,128]{2,1,0:T(8,128)S(1)} %get-tuple-element.170, f32[8]{0:T(128)S(1)} %mul.168, f32[8,128]{1,0:T(8,128)S(1)} %broadcast_multiply_fusion.2), kind=kLoop, calls=%fused_computation.13.clone.1 | loop fusion | flops 3145728 | bytes 1576992 | tf_op jit(solution)/shard_map/convert.1
  134.2 0.2 fusion.35
  134.6 0.6 gather_fusion
  135.2 1.0 fusion.33
  136.5 2.7 %multiply_convert_fusion.3 = (bf16[8,128,128]{2,1,0:T(8,128)(2,1)S(1)}, bf16[8,128,128]{2,1,0:T(8,128)(2,1)S(1)}) fusion(f32[8,128,128]{2,1,0:T(8,128)S(1)} %get-tuple-element.169, f32[8,128,128]{2,1,0:T(8,128)S(1)} %get-tuple-element.170, f32[8]{0:T(128)S(1)} %mul.168, f32[8,128]{1,0:T(8,128)S(1)} %broadcast_multiply_fusion.2), kind=kLoop, calls=%fused_computation.13.clone.1 | loop fusion | flops 3145728 | bytes 1576992 | tf_op jit(solution)/shard_map/convert.1
  139.3 0.2 fusion.35
  139.6 0.6 copy_bitcast_fusion.2
  (203 shorter events, 6.6 us)
Async XLA Ops:
  0.0 2.9 %copy-start.2 = (s32[1,8,8]{2,1,0:T(8,128)S(1)}, s32[1,8,8]{2,1,0:T(8,128)}, u32[]{:S(2)}) copy-start(s32[1,8,8]{2,1,0:T(8,128)} %param.16) | copy-start | bytes 772
  3.7 0.7 copy-start.5
  9.1 7.3 %copy-start.1 = (s32[4]{0:T(128)S(1)}, s32[4]{0:T(128)}, u32[]{:S(2)}) copy-start(s32[4]{0:T(128)} %param.18) | copy-start | bytes 52
  9.1 8.6 %copy-start.3 = (s32[4,24]{1,0:T(4,128)S(1)}, s32[4,24]{1,0:T(4,128)}, u32[]{:S(2)}) copy-start(s32[4,24]{1,0:T(4,128)} %param.17) | copy-start | bytes 1156
  9.1 8.7 %copy-start.4 = (s32[4,24]{1,0:T(4,128)S(1)}, s32[4,24]{1,0:T(4,128)}, u32[]{:S(2)}) copy-start(s32[4,24]{1,0:T(4,128)} %param.19) | copy-start | bytes 1156
  9.1 8.8 %copy-start = (f32[3,512]{1,0:T(4,128)S(1)}, f32[3,512]{1,0:T(4,128)}, u32[]{:S(2)}) copy-start(f32[3,512]{1,0:T(4,128)} %param.11) | copy-start | bytes 18436
  9.1 65.3 %all-to-all-start = ((f32[16,8,39,128]{3,1,2,0:T(8,128)}), f32[16,8,39,128]{3,1,2,0:T(8,128)S(1)}, u32[]{:S(2)}, u32[]{:S(2)}) async-start(f32[16,8,39,128]{3,1,2,0:T(8,128)} %scatter_fusion), calls=%async_computation | async-start | bytes 5111808 | tf_op jit(solution)/shard_map/all_to_all | solution.py:56
where the time goes:
time: 141 us; the launch traced here: 140 us
  waiting for transfers between devices  56.5 us (40%)
  other arithmetic  49.6 us (35%)
  local copies, waits for them, and re-layouts  20.4 us (14%)
  starting transfers between devices  7.27 us (5%)
  matrix products  2.4 us (2%)
  blocking collectives  1.92 us (1%)
    all_to_all x1, waiting for transfers between devices, shards(): lax.all_to_all(send_slots, 'dom', split_axis=0, concat_axis=0, tiled=True)  56.5 us
    another operation x24, other arithmetic  32.7 us
    reduce_sum x12, other arithmetic, build_kernel(): normal_part = jnp.sum(offset * source[:, 3:6, :, None], axis=1) * inverse  12.4 us
    all_to_all x1, starting transfers between devices, shards(): lax.all_to_all(send_slots, 'dom', split_axis=0, concat_axis=0, tiled=True)  7.27 us
    gather x12, local copies, waits for them, and re-layouts, add_pair(): source = source_pool[pick_idx]  6.7 us
    gather x2, local copies, waits for them, and re-layouts, shards(): band_tiles = arrived[my_partners]  3.14 us
    scatter x1, local copies, waits for them, and re-layouts, shards(): send_slots = send_slots.at[my_partners].set(part_tiles[band_list[0]])  3.05 us
  transfers between devices with their start and end apart: 1, of which 1 were waited for; matrix products, arithmetic and copies ran while one was open for 1% of the time, Pallas kernels for 0%

commit v1 on v0

--- a/solution.py
+++ b/solution.py
@@ -9,6 +9,29 @@
 coupling = 1.5
 narrow_core = 0.1
 wide_core = 0.4
+
+
+def cut_along(x, dim, size):
+    shape = x.shape
+    pieces = x.reshape(*shape[:dim], size, shape[dim] // size, *shape[dim + 1 :])
+    return jnp.moveaxis(pieces, dim, 0)
+
+
+def laid_out(blocks, dim):
+    blocks = jnp.moveaxis(blocks, 0, dim)
+    dims = blocks.shape
+    return blocks.reshape(*dims[:dim], dims[dim] * dims[dim + 1], *dims[dim + 2 :])
+
+
+def rotated_exchange(x, axis, split_dim, concat_dim):
+    size, here = (lax.axis_size(axis), lax.axis_index(axis))
+    blocks = cut_along(x, split_dim, size)
+    finished = [blocks[here]]
+    for step in range(1, size):
+        sent = blocks[(here + step) % size]
+        finished.append(lax.ppermute(sent, axis, [(i, (i + step) % size) for i in range(size)]))
+    blocks = jnp.stack(finished)[(here - jnp.arange(size)) % size]
+    return laid_out(blocks, concat_dim)
 
 
 def build_kernel(target_pos, source, valid_mask, flag_row):
@@ -53,7 +76,7 @@
     my_partners = partners[0]
     send_slots = jnp.zeros((n_dom, band_size, channels, TILE), jnp.float32)
     send_slots = send_slots.at[my_partners].set(part_tiles[band_list[0]])
-    arrived = lax.all_to_all(send_slots, "dom", split_axis=0, concat_axis=0, tiled=True)
+    arrived = rotated_exchange(send_slots, "dom", 0, 0)
     band_tiles = arrived[my_partners]
     source_pool = jnp.concatenate([part_tiles, band_tiles.reshape(-1, channels, TILE)], axis=0)
     target_pos = positions.reshape(3, local_tiles, TILE).transpose(1, 0, 2)

time: 141 us -> 151 us (1.071)
  starting transfers between devices: 7.27 us -> 54.1 us
  waiting for transfers between devices: 56.5 us -> 11.3 us
  local copies, waits for them, and re-layouts: 20.4 us -> 26.3 us
  other arithmetic: 49.6 us -> 52.2 us
    all_to_all x1 -> x0, waiting for transfers between devices: 56.5 us -> none  [shards(): lax.all_to_all(send_slots, 'dom', split_axis=0, concat_axis=0, tiled=True)]
    ppermute x0 -> x15, starting transfers between devices: none -> 54.1 us  [rotated_exchange(): lax.ppermute(sent, axis, [(i, (i + step) % size) for i in range(size)])]
    ppermute x0 -> x15, waiting for transfers between devices: none -> 11.3 us  [rotated_exchange(): lax.ppermute(sent, axis, [(i, (i + step) % size) for i in range(size)])]
    all_to_all x1 -> x0, starting transfers between devices: 7.27 us -> none  [shards(): lax.all_to_all(send_slots, 'dom', split_axis=0, concat_axis=0, tiled=True)]
    gather x0 -> x1, local copies, waits for them, and re-layouts: none -> 2.55 us  [rotated_exchange(): blocks = jnp.stack(finished)[(here - jnp.arange(size)) % size]]
    unnamed x13 -> x32, local copies, waits for them, and re-layouts: 0.46 us -> 2.86 us
  transfers between devices with their start and end apart: 1 -> 15, of which waited for: 1 -> 5; matrix products, arithmetic and copies ran while one was open for 1% -> 2% of each run, Pallas kernels for 0% -> 0%
where the time goes in v1:
time: 151 us; the launch traced here: 150 us
  starting transfers between devices  54.1 us (36%)
  other arithmetic  52.2 us (35%)
  local copies, waits for them, and re-layouts  26.3 us (17%)
  waiting for transfers between devices  11.3 us (7%)
  matrix products  2.37 us (2%)
  blocking collectives  1.92 us (1%)
    ppermute x15, starting transfers between devices, rotated_exchange(): lax.ppermute(sent, axis, [(i, (i + step) % size) for i in range(size)])  54.1 us
    another operation x24, other arithmetic  32.7 us
    reduce_sum x12, other arithmetic, build_kernel(): normal_part = jnp.sum(offset * source[:, 3:6, :, None], axis=1) * inverse  12.4 us
    ppermute x15, waiting for transfers between devices, rotated_exchange(): lax.ppermute(sent, axis, [(i, (i + step) % size) for i in range(size)])  11.3 us
    gather x12, local copies, waits for them, and re-layouts, add_pair(): source = source_pool[pick_idx]  6.7 us
    gather x2, local copies, waits for them, and re-layouts, shards(): band_tiles = arrived[my_partners]  3.29 us
  transfers between devices with their start and end apart: 15, of which 5 were waited for; matrix products, arithmetic and copies ran while one was open for 2% of the time, Pallas kernels for 0%

profile of v1, /device:TPU:16, one launch (start us, length us, event | category | flops | bytes accessed | tf_op | source)
XLA Modules:
  0.0 150.4 jit_solution(10772825123293682779)
XLA Ops:
  0.0 0.7 fusion.20
  0.7 0.7 compare_select_fusion.2
  1.4 0.9 pad_maximum_fusion.1
  2.3 1.9 %all_gather.3 = f32[39,1024]{1,0:T(8,128)S(1)} all-gather(f32[39,512]{1,0:T(8,128)S(1)} %pad_maximum_fusion.1), channel_id=1, replica_groups=mesh['dom'=16,'tgt'=2] {'tgt'}, dimensions={1}, use_global_device_ids=true | all-gather | bytes 239616 | tf_op jit(solution)/shard_map/all_gather | solution.py:72
  4.3 0.6 pad_clamp_fusion.1
  4.9 0.7 gather_fusion.1
  5.6 1.3 copy.29
  7.1 2.1 %scatter_fusion = f32[16,8,39,128]{3,1,2,0:T(8,128)S(1)} fusion(f32[16,8,39,128]{3,1,2,0:T(8,128)S(1)} %broadcast_in_dim.16, s32[8]{0:T(128)S(1)} %fusion.20, f32[8,8,39,128]{3,1,2,0:T(8,128)} %copy.29), kind=kCustom, calls=%fused_computation.4 | custom fusion | bytes 3833888 | tf_op jit(solution)/shard_map/scatter | solution.py:78
  9.2 1.4 constant_dynamic-slice_fusion
  10.7 1.5 collective-permute-start
  12.2 1.5 %collective-permute-start.1 = (f32[1,8,39,128]{3,1,2,0:T(8,128)}, f32[1,8,39,128]{3,1,2,0:T(8,128)S(1)}, u32[]{:S(2)}, u32[]{:S(2)}) collective-permute-start(f32[1,8,39,128]{3,1,2,0:T(8,128)} %get-tuple-element.119), channel_id=1, source_target_pairs={{0,4},{2,6},{4,8},{6,10},{8,12},{10,14},{12,16},{14,18},{16,20},{1... | collective-permute-start | bytes 479240 | tf_op jit(solution)/shard_map/ppermute | solution.py:32
  13.7 2.4 %collective-permute-start.2 = (f32[1,8,39,128]{3,1,2,0:T(8,128)}, f32[1,8,39,128]{3,1,2,0:T(8,128)S(1)}, u32[]{:S(2)}, u32[]{:S(2)}) collective-permute-start(f32[1,8,39,128]{3,1,2,0:T(8,128)} %get-tuple-element.118), channel_id=1, source_target_pairs={{0,6},{2,8},{4,10},{6,12},{8,14},{10,16},{12,18},{14,20},{16,22},{... | collective-permute-start | bytes 479240 | tf_op jit(solution)/shard_map/ppermute | solution.py:32
  16.3 1.6 %collective-permute-start.4 = (f32[1,8,39,128]{3,1,2,0:T(8,128)}, f32[1,8,39,128]{3,1,2,0:T(8,128)S(1)}, u32[]{:S(2)}, u32[]{:S(2)}) collective-permute-start(f32[1,8,39,128]{3,1,2,0:T(8,128)} %get-tuple-element.116), channel_id=1, source_target_pairs={{0,10},{2,12},{4,14},{6,16},{8,18},{10,20},{12,22},{14,24},{16,26}... | collective-permute-start | bytes 479240 | tf_op jit(solution)/shard_map/ppermute | solution.py:32
  18.0 0.6 pad_clamp_fusion.2
  18.6 0.6 reduce_max.9
  19.9 0.8 copy.34
  20.7 0.9 collective-permute-done
  21.6 2.1 %collective-permute-start.5 = (f32[1,8,39,128]{3,1,2,0:T(8,128)}, f32[1,8,39,128]{3,1,2,0:T(8,128)S(1)}, u32[]{:S(2)}, u32[]{:S(2)}) collective-permute-start(f32[1,8,39,128]{3,1,2,0:T(8,128)} %get-tuple-element.115), channel_id=1, source_target_pairs={{0,12},{2,14},{4,16},{6,18},{8,20},{10,22},{12,24},{14,26},{16,28}... | collective-permute-start | bytes 479240 | tf_op jit(solution)/shard_map/ppermute | solution.py:32
  23.7 0.9 bitcast_dynamic-update-slice_fusion.14
  24.7 1.7 %collective-permute-start.6 = (f32[1,8,39,128]{3,1,2,0:T(8,128)}, f32[1,8,39,128]{3,1,2,0:T(8,128)S(1)}, u32[]{:S(2)}, u32[]{:S(2)}) collective-permute-start(f32[1,8,39,128]{3,1,2,0:T(8,128)} %get-tuple-element.114), channel_id=1, source_target_pairs={{0,14},{2,16},{4,18},{6,20},{8,22},{10,24},{12,26},{14,28},{16,30}... | collective-permute-start | bytes 479240 | tf_op jit(solution)/shard_map/ppermute | solution.py:32
  26.4 2.7 %collective-permute-start.7 = (f32[1,8,39,128]{3,1,2,0:T(8,128)}, f32[1,8,39,128]{3,1,2,0:T(8,128)S(1)}, u32[]{:S(2)}, u32[]{:S(2)}) collective-permute-start(f32[1,8,39,128]{3,1,2,0:T(8,128)} %get-tuple-element.113), channel_id=1, source_target_pairs={{0,16},{2,18},{4,20},{6,22},{8,24},{10,26},{12,28},{14,30},{16,0},... | collective-permute-start | bytes 479240 | tf_op jit(solution)/shard_map/ppermute | solution.py:32
  29.3 5.6 %collective-permute-done.4 = f32[1,8,39,128]{3,1,2,0:T(8,128)S(1)} collective-permute-done((f32[1,8,39,128]{3,1,2,0:T(8,128)}, f32[1,8,39,128]{3,1,2,0:T(8,128)S(1)}, u32[]{:S(2)}, u32[]{:S(2)}) %collective-permute-start.4) | collective-permute-done | bytes 159776 | tf_op jit(solution)/shard_map/ppermute | solution.py:32
  34.9 22.7 %collective-permute-start.9 = (f32[1,8,39,128]{3,1,2,0:T(8,128)}, f32[1,8,39,128]{3,1,2,0:T(8,128)S(1)}, u32[]{:S(2)}, u32[]{:S(2)}) collective-permute-start(f32[1,8,39,128]{3,1,2,0:T(8,128)} %get-tuple-element.111), channel_id=1, source_target_pairs={{0,20},{2,22},{4,24},{6,26},{8,28},{10,30},{12,0},{14,2},{16,4},{1... | collective-permute-start | bytes 479240 | tf_op jit(solution)/shard_map/ppermute | solution.py:32
  57.8 5.7 %collective-permute-start.12 = (f32[1,8,39,128]{3,1,2,0:T(8,128)S(1)}, f32[1,8,39,128]{3,1,2,0:T(8,128)S(1)}, u32[]{:S(2)}, u32[]{:S(2)}) collective-permute-start(f32[1,8,39,128]{3,1,2,0:T(8,128)S(1)} %copy-done.3), channel_id=1, source_target_pairs={{0,26},{2,28},{4,30},{6,0},{8,2},{10,4},{12,6},{14,8},{16,10},{18,... | collective-permute-start | bytes 479240 | tf_op jit(solution)/shard_map/ppermute | solution.py:32
  63.5 6.8 %collective-permute-start.13 = (f32[1,8,39,128]{3,1,2,0:T(8,128)S(1)}, f32[1,8,39,128]{3,1,2,0:T(8,128)S(1)}, u32[]{:S(2)}, u32[]{:S(2)}) collective-permute-start(f32[1,8,39,128]{3,1,2,0:T(8,128)S(1)} %copy-done.2), channel_id=1, source_target_pairs={{0,28},{2,30},{4,0},{6,2},{8,4},{10,6},{12,8},{14,10},{16,12},{18,... | collective-permute-start | bytes 479240 | tf_op jit(solution)/shard_map/ppermute | solution.py:32
  70.4 4.8 %collective-permute-start.14 = (f32[1,8,39,128]{3,1,2,0:T(8,128)S(1)}, f32[1,8,39,128]{3,1,2,0:T(8,128)S(1)}, u32[]{:S(2)}, u32[]{:S(2)}) collective-permute-start(f32[1,8,39,128]{3,1,2,0:T(8,128)S(1)} %copy-done.1), channel_id=1, source_target_pairs={{0,30},{2,0},{4,2},{6,4},{8,6},{10,8},{12,10},{14,12},{16,14},{18,... | collective-permute-start | bytes 479240 | tf_op jit(solution)/shard_map/ppermute | solution.py:32
  75.3 1.4 collective-permute-done.12
  76.8 1.7 %collective-permute-done.13 = f32[1,8,39,128]{3,1,2,0:T(8,128)S(1)} collective-permute-done((f32[1,8,39,128]{3,1,2,0:T(8,128)S(1)}, f32[1,8,39,128]{3,1,2,0:T(8,128)S(1)}, u32[]{:S(2)}, u32[]{:S(2)}) %collective-permute-start.13) | collective-permute-done | bytes 159776 | tf_op jit(solution)/shard_map/ppermute | solution.py:32
  78.5 1.7 %collective-permute-done.14 = f32[1,8,39,128]{3,1,2,0:T(8,128)S(1)} collective-permute-done((f32[1,8,39,128]{3,1,2,0:T(8,128)S(1)}, f32[1,8,39,128]{3,1,2,0:T(8,128)S(1)}, u32[]{:S(2)}, u32[]{:S(2)}) %collective-permute-start.14) | collective-permute-done | bytes 159776 | tf_op jit(solution)/shard_map/ppermute | solution.py:32
  80.2 1.5 copy-done
  81.7 2.6 %gather_fusion.2 = f32[16,8,39,128]{3,1,2,0:T(8,128)S(1)} fusion(f32[16,8,39,128]{3,1,2,0:T(8,128)} %bitcast.83, s32[1024]{0:T(1024)} %pad_clamp_fusion.2), kind=kCustom, calls=%fused_computation.2 | custom fusion | bytes 5111872 | tf_op jit(solution)/shard_map/gather | solution.py:33
  84.2 1.8 %gather_fusion.3 = f32[8,8,39,128]{3,1,2,0:T(8,128)} fusion(f32[16,8,39,128]{3,1,2,0:T(8,128)S(1)} %gather_fusion.2, s32[1024]{0:T(1024)} %get-tuple-element.123), kind=kCustom, calls=%fused_computation.3 | custom fusion | bytes 2555936 | tf_op jit(solution)/shard_map/gather | solution.py:80
  86.1 1.5 copy.42
  88.2 61.6 %while.10 = (s32[]{:T(128)}, f32[4,32,128]{2,1,0:T(8,128)S(1)}, s32[]{:T(128)}, s32[4,24]{0,1:T(8,128)S(1)}, f32[72,39,128]{2,1,0:T(8,128)S(1)}, /*index=5*/s32[...) while((s32[]{:T(128)}, f32[4,32,128]{2,1,0:T(8,128)S(1)}, ...), condition=%wide.region_5.6_spmd, body=%wide.region_2.5_spmd.sunk | while | flops 23290952 | bytes 4471535 | solution.py:101
  88.9 1.0 fusion.35
  90.3 2.7 %multiply_convert_fusion.3 = (bf16[8,128,128]{2,1,0:T(8,128)(2,1)S(1)}, bf16[8,128,128]{2,1,0:T(8,128)(2,1)S(1)}) fusion(f32[8,128,128]{2,1,0:T(8,128)S(1)} %get-tuple-element.186, f32[8,128,128]{2,1,0:T(8,128)S(1)} %get-tuple-element.187, f32[8]{0:T(128)S(1)} %mul.168, f32[8,128]{1,0:T(8,128)S(1)} %broadcast_multiply_fusion.2), kind=kLoop, calls=%fused_computation.14.clone.1 | loop fusion | flops 3145728 | bytes 1576992 | tf_op jit(solution)/shard_map/convert.1
  93.4 0.6 gather_fusion
  94.0 1.0 fusion.35
  95.4 2.7 %multiply_convert_fusion.3 = (bf16[8,128,128]{2,1,0:T(8,128)(2,1)S(1)}, bf16[8,128,128]{2,1,0:T(8,128)(2,1)S(1)}) fusion(f32[8,128,128]{2,1,0:T(8,128)S(1)} %get-tuple-element.186, f32[8,128,128]{2,1,0:T(8,128)S(1)} %get-tuple-element.187, f32[8]{0:T(128)S(1)} %mul.168, f32[8,128]{1,0:T(8,128)S(1)} %broadcast_multiply_fusion.2), kind=kLoop, calls=%fused_computation.14.clone.1 | loop fusion | flops 3145728 | bytes 1576992 | tf_op jit(solution)/shard_map/convert.1
  99.2 1.0 fusion.35
  100.5 2.7 %multiply_convert_fusion.3 = (bf16[8,128,128]{2,1,0:T(8,128)(2,1)S(1)}, bf16[8,128,128]{2,1,0:T(8,128)(2,1)S(1)}) fusion(f32[8,128,128]{2,1,0:T(8,128)S(1)} %get-tuple-element.186, f32[8,128,128]{2,1,0:T(8,128)S(1)} %get-tuple-element.187, f32[8]{0:T(128)S(1)} %mul.168, f32[8,128]{1,0:T(8,128)S(1)} %broadcast_multiply_fusion.2), kind=kLoop, calls=%fused_computation.14.clone.1 | loop fusion | flops 3145728 | bytes 1576992 | tf_op jit(solution)/shard_map/convert.1
  104.3 1.0 fusion.35
  105.7 2.7 %multiply_convert_fusion.3 = (bf16[8,128,128]{2,1,0:T(8,128)(2,1)S(1)}, bf16[8,128,128]{2,1,0:T(8,128)(2,1)S(1)}) fusion(f32[8,128,128]{2,1,0:T(8,128)S(1)} %get-tuple-element.186, f32[8,128,128]{2,1,0:T(8,128)S(1)} %get-tuple-element.187, f32[8]{0:T(128)S(1)} %mul.168, f32[8,128]{1,0:T(8,128)S(1)} %broadcast_multiply_fusion.2), kind=kLoop, calls=%fused_computation.14.clone.1 | loop fusion | flops 3145728 | bytes 1576992 | tf_op jit(solution)/shard_map/convert.1
  109.4 1.0 fusion.35
  110.8 2.7 %multiply_convert_fusion.3 = (bf16[8,128,128]{2,1,0:T(8,128)(2,1)S(1)}, bf16[8,128,128]{2,1,0:T(8,128)(2,1)S(1)}) fusion(f32[8,128,128]{2,1,0:T(8,128)S(1)} %get-tuple-element.186, f32[8,128,128]{2,1,0:T(8,128)S(1)} %get-tuple-element.187, f32[8]{0:T(128)S(1)} %mul.168, f32[8,128]{1,0:T(8,128)S(1)} %broadcast_multiply_fusion.2), kind=kLoop, calls=%fused_computation.14.clone.1 | loop fusion | flops 3145728 | bytes 1576992 | tf_op jit(solution)/shard_map/convert.1
  114.0 0.6 gather_fusion
  114.6 1.0 fusion.35
  116.0 2.7 %multiply_convert_fusion.3 = (bf16[8,128,128]{2,1,0:T(8,128)(2,1)S(1)}, bf16[8,128,128]{2,1,0:T(8,128)(2,1)S(1)}) fusion(f32[8,128,128]{2,1,0:T(8,128)S(1)} %get-tuple-element.186, f32[8,128,128]{2,1,0:T(8,128)S(1)} %get-tuple-element.187, f32[8]{0:T(128)S(1)} %mul.168, f32[8,128]{1,0:T(8,128)S(1)} %broadcast_multiply_fusion.2), kind=kLoop, calls=%fused_computation.14.clone.1 | loop fusion | flops 3145728 | bytes 1576992 | tf_op jit(solution)/shard_map/convert.1
  119.7 1.0 fusion.35
  121.1 2.7 %multiply_convert_fusion.3 = (bf16[8,128,128]{2,1,0:T(8,128)(2,1)S(1)}, bf16[8,128,128]{2,1,0:T(8,128)(2,1)S(1)}) fusion(f32[8,128,128]{2,1,0:T(8,128)S(1)} %get-tuple-element.186, f32[8,128,128]{2,1,0:T(8,128)S(1)} %get-tuple-element.187, f32[8]{0:T(128)S(1)} %mul.168, f32[8,128]{1,0:T(8,128)S(1)} %broadcast_multiply_fusion.2), kind=kLoop, calls=%fused_computation.14.clone.1 | loop fusion | flops 3145728 | bytes 1576992 | tf_op jit(solution)/shard_map/convert.1
  124.3 0.6 gather_fusion
  124.8 1.0 fusion.35
  126.2 2.7 %multiply_convert_fusion.3 = (bf16[8,128,128]{2,1,0:T(8,128)(2,1)S(1)}, bf16[8,128,128]{2,1,0:T(8,128)(2,1)S(1)}) fusion(f32[8,128,128]{2,1,0:T(8,128)S(1)} %get-tuple-element.186, f32[8,128,128]{2,1,0:T(8,128)S(1)} %get-tuple-element.187, f32[8]{0:T(128)S(1)} %mul.168, f32[8,128]{1,0:T(8,128)S(1)} %broadcast_multiply_fusion.2), kind=kLoop, calls=%fused_computation.14.clone.1 | loop fusion | flops 3145728 | bytes 1576992 | tf_op jit(solution)/shard_map/convert.1
  130.0 1.0 fusion.35
  131.4 2.7 %multiply_convert_fusion.3 = (bf16[8,128,128]{2,1,0:T(8,128)(2,1)S(1)}, bf16[8,128,128]{2,1,0:T(8,128)(2,1)S(1)}) fusion(f32[8,128,128]{2,1,0:T(8,128)S(1)} %get-tuple-element.186, f32[8,128,128]{2,1,0:T(8,128)S(1)} %get-tuple-element.187, f32[8]{0:T(128)S(1)} %mul.168, f32[8,128]{1,0:T(8,128)S(1)} %broadcast_multiply_fusion.2), kind=kLoop, calls=%fused_computation.14.clone.1 | loop fusion | flops 3145728 | bytes 1576992 | tf_op jit(solution)/shard_map/convert.1
  134.5 0.6 gather_fusion
  135.1 1.0 fusion.35
  136.5 2.7 %multiply_convert_fusion.3 = (bf16[8,128,128]{2,1,0:T(8,128)(2,1)S(1)}, bf16[8,128,128]{2,1,0:T(8,128)(2,1)S(1)}) fusion(f32[8,128,128]{2,1,0:T(8,128)S(1)} %get-tuple-element.186, f32[8,128,128]{2,1,0:T(8,128)S(1)} %get-tuple-element.187, f32[8]{0:T(128)S(1)} %mul.168, f32[8,128]{1,0:T(8,128)S(1)} %broadcast_multiply_fusion.2), kind=kLoop, calls=%fused_computation.14.clone.1 | loop fusion | flops 3145728 | bytes 1576992 | tf_op jit(solution)/shard_map/convert.1
  139.7 0.6 gather_fusion
  140.2 1.0 fusion.35
  141.6 2.7 %multiply_convert_fusion.3 = (bf16[8,128,128]{2,1,0:T(8,128)(2,1)S(1)}, bf16[8,128,128]{2,1,0:T(8,128)(2,1)S(1)}) fusion(f32[8,128,128]{2,1,0:T(8,128)S(1)} %get-tuple-element.186, f32[8,128,128]{2,1,0:T(8,128)S(1)} %get-tuple-element.187, f32[8]{0:T(128)S(1)} %mul.168, f32[8,128]{1,0:T(8,128)S(1)} %broadcast_multiply_fusion.2), kind=kLoop, calls=%fused_computation.14.clone.1 | loop fusion | flops 3145728 | bytes 1576992 | tf_op jit(solution)/shard_map/convert.1
  145.4 1.0 fusion.35
  146.8 2.7 %multiply_convert_fusion.3 = (bf16[8,128,128]{2,1,0:T(8,128)(2,1)S(1)}, bf16[8,128,128]{2,1,0:T(8,128)(2,1)S(1)}) fusion(f32[8,128,128]{2,1,0:T(8,128)S(1)} %get-tuple-element.186, f32[8,128,128]{2,1,0:T(8,128)S(1)} %get-tuple-element.187, f32[8]{0:T(128)S(1)} %mul.168, f32[8,128]{1,0:T(8,128)S(1)} %broadcast_multiply_fusion.2), kind=kLoop, calls=%fused_computation.14.clone.1 | loop fusion | flops 3145728 | bytes 1576992 | tf_op jit(solution)/shard_map/convert.1
  149.8 0.6 copy_bitcast_fusion.2
  (254 shorter events, 14.3 us)
Async XLA Ops:
  9.2 8.8 %copy-start.4 = (f32[3,512]{1,0:T(4,128)S(1)}, f32[3,512]{1,0:T(4,128)}, u32[]{:S(2)}) copy-start(f32[3,512]{1,0:T(4,128)} %param.11) | copy-start | bytes 18436
  9.2 9.4 %copy-start.5 = (s32[4]{0:T(128)S(1)}, s32[4]{0:T(128)}, u32[]{:S(2)}) copy-start(s32[4]{0:T(128)} %param.18) | copy-start | bytes 52
  9.2 10.6 %copy-start.7 = (s32[4,24]{1,0:T(4,128)S(1)}, s32[4,24]{1,0:T(4,128)}, u32[]{:S(2)}) copy-start(s32[4,24]{1,0:T(4,128)} %param.17) | copy-start | bytes 1156
  10.7 11.0 %collective-permute-start = (f32[1,8,39,128]{3,1,2,0:T(8,128)}, f32[1,8,39,128]{3,1,2,0:T(8,128)}, u32[]{:S(2)}, u32[]{:S(2)}) collective-permute-start(f32[1,8,39,128]{3,1,2,0:T(8,128)} %get-tuple-element.120), channel_id=1, source_target_pairs={{0,2},{2,4},{4,6},{6,8},{8,10},{10,12},{12,14},{14,16},{16,18},{18... | collective-permute-start | bytes 479240 | tf_op jit(solution)/shard_map/ppermute | solution.py:32
  12.2 12.5 %collective-permute-start.1 = (f32[1,8,39,128]{3,1,2,0:T(8,128)}, f32[1,8,39,128]{3,1,2,0:T(8,128)S(1)}, u32[]{:S(2)}, u32[]{:S(2)}) collective-permute-start(f32[1,8,39,128]{3,1,2,0:T(8,128)} %get-tuple-element.119), channel_id=1, source_target_pairs={{0,4},{2,6},{4,8},{6,10},{8,12},{10,14},{12,16},{14,18},{16,20},{1... | collective-permute-start | bytes 479240 | tf_op jit(solution)/shard_map/ppermute | solution.py:32
  13.7 12.7 %collective-permute-start.2 = (f32[1,8,39,128]{3,1,2,0:T(8,128)}, f32[1,8,39,128]{3,1,2,0:T(8,128)S(1)}, u32[]{:S(2)}, u32[]{:S(2)}) collective-permute-start(f32[1,8,39,128]{3,1,2,0:T(8,128)} %get-tuple-element.118), channel_id=1, source_target_pairs={{0,6},{2,8},{4,10},{6,12},{8,14},{10,16},{12,18},{14,20},{16,22},{... | collective-permute-start | bytes 479240 | tf_op jit(solution)/shard_map/ppermute | solution.py:32
  16.1 13.0 %collective-permute-start.3 = (f32[1,8,39,128]{3,1,2,0:T(8,128)}, f32[1,8,39,128]{3,1,2,0:T(8,128)S(1)}, u32[]{:S(2)}, u32[]{:S(2)}) collective-permute-start(f32[1,8,39,128]{3,1,2,0:T(8,128)} %get-tuple-element.117), channel_id=1, source_target_pairs={{0,8},{2,10},{4,12},{6,14},{8,16},{10,18},{12,20},{14,22},{16,24},... | collective-permute-start | bytes 479240 | tf_op jit(solution)/shard_map/ppermute | solution.py:32
  16.3 18.5 %collective-permute-start.4 = (f32[1,8,39,128]{3,1,2,0:T(8,128)}, f32[1,8,39,128]{3,1,2,0:T(8,128)S(1)}, u32[]{:S(2)}, u32[]{:S(2)}) collective-permute-start(f32[1,8,39,128]{3,1,2,0:T(8,128)} %get-tuple-element.116), channel_id=1, source_target_pairs={{0,10},{2,12},{4,14},{6,16},{8,18},{10,20},{12,22},{14,24},{16,26}... | collective-permute-start | bytes 479240 | tf_op jit(solution)/shard_map/ppermute | solution.py:32
  20.7 37.1 %copy-start.3 = (f32[1,8,39,128]{3,1,2,0:T(8,128)S(1)}, f32[1,8,39,128]{3,1,2,0:T(8,128)}, u32[]{:S(2)}) copy-start(f32[1,8,39,128]{3,1,2,0:T(8,128)} %get-tuple-element.108) | copy-start | bytes 479236
  20.7 42.8 %copy-start.2 = (f32[1,8,39,128]{3,1,2,0:T(8,128)S(1)}, f32[1,8,39,128]{3,1,2,0:T(8,128)}, u32[]{:S(2)}) copy-start(f32[1,8,39,128]{3,1,2,0:T(8,128)} %get-tuple-element.107) | copy-start | bytes 479236
  20.7 49.7 %copy-start.1 = (f32[1,8,39,128]{3,1,2,0:T(8,128)S(1)}, f32[1,8,39,128]{3,1,2,0:T(8,128)}, u32[]{:S(2)}) copy-start(f32[1,8,39,128]{3,1,2,0:T(8,128)} %get-tuple-element.106) | copy-start | bytes 479236
  21.6 35.9 %collective-permute-start.5 = (f32[1,8,39,128]{3,1,2,0:T(8,128)}, f32[1,8,39,128]{3,1,2,0:T(8,128)S(1)}, u32[]{:S(2)}, u32[]{:S(2)}) collective-permute-start(f32[1,8,39,128]{3,1,2,0:T(8,128)} %get-tuple-element.115), channel_id=1, source_target_pairs={{0,12},{2,14},{4,16},{6,18},{8,20},{10,22},{12,24},{14,26},{16,28}... | collective-permute-start | bytes 479240 | tf_op jit(solution)/shard_map/ppermute | solution.py:32
  24.7 33.0 %collective-permute-start.6 = (f32[1,8,39,128]{3,1,2,0:T(8,128)}, f32[1,8,39,128]{3,1,2,0:T(8,128)S(1)}, u32[]{:S(2)}, u32[]{:S(2)}) collective-permute-start(f32[1,8,39,128]{3,1,2,0:T(8,128)} %get-tuple-element.114), channel_id=1, source_target_pairs={{0,14},{2,16},{4,18},{6,20},{8,22},{10,24},{12,26},{14,28},{16,30}... | collective-permute-start | bytes 479240 | tf_op jit(solution)/shard_map/ppermute | solution.py:32
  26.4 31.3 %collective-permute-start.7 = (f32[1,8,39,128]{3,1,2,0:T(8,128)}, f32[1,8,39,128]{3,1,2,0:T(8,128)S(1)}, u32[]{:S(2)}, u32[]{:S(2)}) collective-permute-start(f32[1,8,39,128]{3,1,2,0:T(8,128)} %get-tuple-element.113), channel_id=1, source_target_pairs={{0,16},{2,18},{4,20},{6,22},{8,24},{10,26},{12,28},{14,30},{16,0},... | collective-permute-start | bytes 479240 | tf_op jit(solution)/shard_map/ppermute | solution.py:32
  29.1 34.4 %collective-permute-start.8 = (f32[1,8,39,128]{3,1,2,0:T(8,128)}, f32[1,8,39,128]{3,1,2,0:T(8,128)S(1)}, u32[]{:S(2)}, u32[]{:S(2)}) collective-permute-start(f32[1,8,39,128]{3,1,2,0:T(8,128)} %get-tuple-element.112), channel_id=1, source_target_pairs={{0,18},{2,20},{4,22},{6,24},{8,26},{10,28},{12,30},{14,0},{16,2},{... | collective-permute-start | bytes 479240 | tf_op jit(solution)/shard_map/ppermute | solution.py:32
  34.9 35.5 %collective-permute-start.9 = (f32[1,8,39,128]{3,1,2,0:T(8,128)}, f32[1,8,39,128]{3,1,2,0:T(8,128)S(1)}, u32[]{:S(2)}, u32[]{:S(2)}) collective-permute-start(f32[1,8,39,128]{3,1,2,0:T(8,128)} %get-tuple-element.111), channel_id=1, source_target_pairs={{0,20},{2,22},{4,24},{6,26},{8,28},{10,30},{12,0},{14,2},{16,4},{1... | collective-permute-start | bytes 479240 | tf_op jit(solution)/shard_map/ppermute | solution.py:32
  57.6 17.7 %collective-permute-start.10 = (f32[1,8,39,128]{3,1,2,0:T(8,128)}, f32[1,8,39,128]{3,1,2,0:T(8,128)S(1)}, u32[]{:S(2)}, u32[]{:S(2)}) collective-permute-start(f32[1,8,39,128]{3,1,2,0:T(8,128)} %get-tuple-element.110), channel_id=1, source_target_pairs={{0,22},{2,24},{4,26},{6,28},{8,30},{10,0},{12,2},{14,4},{16,6},{18... | collective-permute-start | bytes 479240 | tf_op jit(solution)/shard_map/ppermute | solution.py:32
  57.7 17.6 %collective-permute-start.11 = (f32[1,8,39,128]{3,1,2,0:T(8,128)S(1)}, f32[1,8,39,128]{3,1,2,0:T(8,128)S(1)}, u32[]{:S(2)}, u32[]{:S(2)}) collective-permute-start(f32[1,8,39,128]{3,1,2,0:T(8,128)S(1)} %get-tuple-element.109), channel_id=1, source_target_pairs={{0,24},{2,26},{4,28},{6,30},{8,0},{10,2},{12,4},{14,6},{16,8},{18,... | collective-permute-start | bytes 479240 | tf_op jit(solution)/shard_map/ppermute | solution.py:32
  57.8 19.0 %collective-permute-start.12 = (f32[1,8,39,128]{3,1,2,0:T(8,128)S(1)}, f32[1,8,39,128]{3,1,2,0:T(8,128)S(1)}, u32[]{:S(2)}, u32[]{:S(2)}) collective-permute-start(f32[1,8,39,128]{3,1,2,0:T(8,128)S(1)} %copy-done.3), channel_id=1, source_target_pairs={{0,26},{2,28},{4,30},{6,0},{8,2},{10,4},{12,6},{14,8},{16,10},{18,... | collective-permute-start | bytes 479240 | tf_op jit(solution)/shard_map/ppermute | solution.py:32
  63.5 14.9 %collective-permute-start.13 = (f32[1,8,39,128]{3,1,2,0:T(8,128)S(1)}, f32[1,8,39,128]{3,1,2,0:T(8,128)S(1)}, u32[]{:S(2)}, u32[]{:S(2)}) collective-permute-start(f32[1,8,39,128]{3,1,2,0:T(8,128)S(1)} %copy-done.2), channel_id=1, source_target_pairs={{0,28},{2,30},{4,0},{6,2},{8,4},{10,6},{12,8},{14,10},{16,12},{18,... | collective-permute-start | bytes 479240 | tf_op jit(solution)/shard_map/ppermute | solution.py:32
  70.4 9.8 %collective-permute-start.14 = (f32[1,8,39,128]{3,1,2,0:T(8,128)S(1)}, f32[1,8,39,128]{3,1,2,0:T(8,128)S(1)}, u32[]{:S(2)}, u32[]{:S(2)}) collective-permute-start(f32[1,8,39,128]{3,1,2,0:T(8,128)S(1)} %copy-done.1), channel_id=1, source_target_pairs={{0,30},{2,0},{4,2},{6,4},{8,6},{10,8},{12,10},{14,12},{16,14},{18,... | collective-permute-start | bytes 479240 | tf_op jit(solution)/shard_map/ppermute | solution.py:32
  80.2 1.5 copy-start
  87.5 0.7 copy-start.6
